TPU v7x, 32 devices: a whole 2x2x4 slice. The times are simulated.
32 devices in a mesh: row: 8 (over y, x, core), col: 4 (over z).
Axes of the slice: x: 2, y: 2, z: 4, core: 2. Of those that a mesh axis runs over, the one named last changes fastest.
Arguments:
- offsets: float32 [2, 4, 512, 512], P(None, None, 'row', 'col'), may hold values from 0 to 1
- velocity: float32 [2, 4, 512, 512], P(None, None, 'row', 'col'), may hold values from -5 to 5
- mass: float32 [4, 512, 512], P(None, 'row', 'col'), may hold values from 0.5 to 2
- counts: int32 [512, 512], P('row', 'col'), may hold values from 0 to 4
- spectrum_low: float32 [1], replicated, may hold values from 0.5 to 2
- spectrum_high: float32 [1], replicated, may hold values from 10 to 20
Outputs:
- new_velocity: float32 [2, 4, 512, 512], P(None, None, 'row', 'col')
- pressure: float32 [4, 512, 512], P(None, 'row', 'col')
Inputs may be any that keep to these rules, and one draw needn't show every extreme that they name: `counts`: slot s of a cell holds a live particle exactly when s is below the cell's count.
All inputs are finite; a program needn't handle non-finite values.
Results may differ from a plain program's by a relative error of at most 0.0001.
Values sent between devices are 32-bit elements; how exact they have to be, the bound alone decides.
A program may use at most 64 MiB of HBM per device.

v0:
```python
import functools
import math

import jax
import jax.numpy as jnp
from jax import lax
from jax.experimental import pallas as pl
from jax.experimental.pallas import tpu as pltpu
from jax.sharding import PartitionSpec as P

TIME_STEP = 0.1
KERNEL_NORM = 7.0 / (4.0 * math.pi)
SLOPE_NORM = 20.0 * KERNEL_NORM / 4.0
BACKGROUND = 0.5 * KERNEL_NORM
DIAGONAL_SHIFT = 1.0
TINY = 1e-30
MESH = pl.DeviceIdType.MESH
DIRECTIONS = ((1, 0), (-1, 0), (0, 1), (0, -1), (1, 1), (-1, 1), (1, -1), (-1, -1))


def kernel(
    rows,
    cols,
    off_hbm,
    vel_hbm,
    mass_hbm,
    counts_hbm,
    low_hbm,
    high_hbm,
    nv_ref,
    press_ref,
    off_ref,
    vel_ref,
    mass_ref,
    counts_ref,
    low_ref,
    high_ref,
    sums_ref,
    input_sem,
    state_e,
    state_cs,
    state_cr,
    field_e,
    field_cs,
    field_cr,
    near_s,
    near_p,
    slopes_ref,
    own_ref,
    send_sem,
    recv_sem,
):
    slots, height, width = mass_hbm.shape
    steps = height // 8
    my_row = lax.axis_index("row")
    my_col = lax.axis_index("col")

    def exists(dr, dc):
        answer = None
        for shift, place, count in ((dr, my_row, rows), (dc, my_col, cols)):
            if shift == 0:
                continue
            test = place + shift < count if shift > 0 else place + shift >= 0
            answer = test if answer is None else jnp.logical_and(answer, test)
        return answer

    lane = lax.broadcasted_iota(jnp.int32, (8, width), 1)

    exchanges = [(state_e, state_cs, state_cr)] + [
        (field_e.at[n], field_cs.at[n], field_cr.at[n]) for n in range(3)
    ]
    loads = [
        pltpu.make_async_copy(source, target, input_sem.at[n])
        for n, (source, target) in enumerate(
            (
                (counts_hbm, counts_ref),
                (vel_hbm, vel_ref),
                (off_hbm, off_ref),
                (mass_hbm, mass_ref),
                (low_hbm, low_ref),
                (high_hbm, high_ref),
            )
        )
    ]
    for load in loads:
        load.start()

    barrier = pltpu.get_barrier_semaphore()
    for dr, dc in DIRECTIONS:

        @pl.when(exists(dr, dc))
        def _(dr=dr, dc=dc):
            pl.semaphore_signal(
                barrier, inc=1, device_id=(my_row + dr, my_col + dc), device_id_type=MESH
            )

    for e_ref, _, cr_ref in exchanges:
        planes = e_ref.shape[0]
        for dr, begin in ((-1, 0), (1, height + 8)):

            @pl.when(jnp.logical_not(exists(dr, 0)))
            def _(e_ref=e_ref, begin=begin, planes=planes):
                e_ref[:, begin : begin + 8, :] = jnp.zeros((planes, 8, width), jnp.float32)

        for side, dc in ((0, -1), (1, 1)):
            for dr, begin, size in ((-1, 0, 8), (0, 8, height), (1, height + 8, 8)):

                @pl.when(jnp.logical_not(exists(dr, dc)))
                def _(cr_ref=cr_ref, side=side, begin=begin, size=size):
                    cr_ref[side, begin : begin + size, :] = jnp.zeros((size, width), jnp.float32)

    for load in loads:
        load.wait()

    for slot in range(slots):
        occupied = jnp.where(counts_ref[...] > slot, 1.0, 0.0).astype(jnp.float32)
        inner = slice(8, 8 + height)
        for axis in range(2):
            speed = vel_ref[axis, slot]
            state_e[axis * slots + slot, inner, :] = 0.5 * (off_ref[axis, slot] + TIME_STEP * speed)
            state_e[(2 + axis) * slots + slot, inner, :] = speed
        state_e[4 * slots + slot, inner, :] = SLOPE_NORM * (mass_ref[slot] * occupied)

    def pack(e_ref, cs_ref):
        planes = e_ref.shape[0]

        def tile(number, carry):
            begin = number * 8 if isinstance(number, int) else pl.multiple_of(number * 8, 8)
            left = jnp.zeros((8, width), jnp.float32)
            right = jnp.zeros((8, width), jnp.float32)
            for plane in range(planes):
                value = e_ref[plane, pl.ds(begin + 8, 8), :]
                if plane:
                    value = pltpu.roll(value, 4 * plane, 1)
                at = 4 * plane
                left = jnp.where((lane == at) | (lane == at + 1), value, left)
                low = (at - 2) % width
                right = jnp.where((lane == low) | (lane == low + 1), value, right)
            cs_ref[0, pl.ds(begin, 8), :] = left
            cs_ref[1, pl.ds(begin, 8), :] = right
            return carry

        if planes > slots:
            lax.fori_loop(0, steps, tile, 0)
        else:
            for number in range(steps):
                tile(number, 0)

    def copy(number, way):
        e_ref, cs_ref, cr_ref = exchanges[number]
        dr, dc = DIRECTIONS[way]
        if dc == 0:
            if dr > 0:
                source, target = e_ref.at[:, height : height + 8, :], e_ref.at[:, 0:8, :]
            else:
                source = e_ref.at[:, 8:16, :]
                target = e_ref.at[:, height + 8 : height + 16, :]
        else:
            mine, theirs = (1, 0) if dc > 0 else (0, 1)
            if dr == 0:
                source, target = cs_ref.at[mine], cr_ref.at[theirs, 8 : 8 + height, :]
            elif dr > 0:
                source = cs_ref.at[mine, height - 8 : height, :]
                target = cr_ref.at[theirs, 0:8, :]
            else:
                source = cs_ref.at[mine, 0:8, :]
                target = cr_ref.at[theirs, height + 8 : height + 16, :]
        return pltpu.make_async_remote_copy(
            src_ref=source,
            dst_ref=target,
            send_sem=send_sem.at[number, way],
            recv_sem=recv_sem.at[number, way],
            device_id=(my_row + dr, my_col + dc),
            device_id_type=MESH,
        )

    def send(number):
        for way in (4, 5, 6, 7, 2, 3, 0, 1):

            @pl.when(exists(*DIRECTIONS[way]))
            def _(way=way):
                copy(number, way).start()

    def receive(number, ways):
        for way in ways:
            dr, dc = DIRECTIONS[way]

            @pl.when(exists(-dr, -dc))
            def _(way=way):
                copy(number, way).wait_recv()

    def drain(number):
        for way in range(8):

            @pl.when(exists(*DIRECTIONS[way]))
            def _(way=way):
                copy(number, way).wait_send()

    def spread(number, near_ref, k, shifts):
        e_ref, _, cr_ref = exchanges[number]
        planes = e_ref.shape[0]
        lines = pl.ds(6 + k, 8, stride=8)
        if shifts != (0,):
            rim = cr_ref[0, lines, :] + cr_ref[1, lines, :]
        for plane in range(planes):
            value = e_ref[plane, lines, :]
            along = planes > slots and slots <= plane < 2 * slots
            for shift in shifts:
                moved = value
                if shift:
                    rolled = pltpu.roll(value, -shift % width, 1)
                    edge = pltpu.roll(rim, (-4 * plane - shift) % width, 1) if 4 * plane + shift else rim
                    inner = lane < width - shift if shift > 0 else lane >= -shift
                    moved = jnp.where(inner, rolled, edge)
                if along and shift:
                    moved = moved + 0.5 * shift
                near_ref[shift + 2, plane, k] = moved

    def spread_lines(number, near_ref, begins, shifts):
        first, gap, count = begins

        def lines(index, carry):
            for k in range(2):
                spread(number, near_ref, first + index * gap + k, shifts)
            return carry

        if near_ref.shape[1] > slots:
            lax.fori_loop(0, count, lines, 0)
        else:
            for index in range(count):
                lines(index, 0)

    inside = (2, 2, steps // 2)
    outside = (0, steps + 2, 2)
    beside = (-2, -1, 1, 2)
    everywhere = (-2, -1, 0, 1, 2)

    def inner_lines(work):
        def body(t, carry):
            work(t)
            return carry

        lax.fori_loop(2, steps - 2, body, 0)

    def outer_lines(work):
        def body(index, carry):
            work(index + (index // 2) * (steps - 4))
            return carry

        lax.fori_loop(0, 4, body, 0)

    pack(state_e, state_cs)
    tall = 1 + jnp.where(my_row > 0, 1, 0) + jnp.where(my_row + 1 < rows, 1, 0)
    wide = 1 + jnp.where(my_col > 0, 1, 0) + jnp.where(my_col + 1 < cols, 1, 0)
    pl.semaphore_wait(barrier, tall * wide - 1)

    send(0)
    spread_lines(0, near_s, inside, (0,))

    full = (8, width)
    low = jnp.broadcast_to(low_ref[0], full)
    high = jnp.broadcast_to(high_ref[0], full)
    middle = 0.5 * (high + low)
    radius = 0.5 * (high - low)
    quotient = middle / radius
    factor_zero = 1.0 / quotient
    factor_one = 1.0 / (2.0 * quotient - factor_zero)
    factor_two = 1.0 / (2.0 * quotient - factor_one)
    over_middle = 1.0 / middle
    keep_one = factor_one * factor_zero
    keep_two = factor_two * factor_one
    gain_one = 2.0 * factor_one / radius
    gain_two = 2.0 * factor_two / radius

    def own_state(field, t):
        return near_s[2, field * slots : (field + 1) * slots, t + 2]

    def put_field(number, t, value):
        for slot in range(slots):
            field_e[number, slot, pl.ds(8 + t, 8, stride=8), :] = value[slot]

    zero = jnp.zeros((slots, 8, width), jnp.float32)

    def flow(t, shifts, sums):
        own_x = own_state(0, t)
        own_y = own_state(1, t)
        own_vx = own_state(2, t)
        own_vy = own_state(3, t)

        def along(e, sums):
            dens, inflow, slope_sum = sums
            base_x = own_x - 0.5 * jnp.asarray(e - 2, jnp.float32)
            for f in shifts:
                for b in range(slots):
                    dx = near_s[f, b, t + e][None] - base_x
                    dy = near_s[f, slots + b, t + e][None] - own_y
                    square = dx * dx + dy * dy
                    q = square * lax.rsqrt(jnp.maximum(square, TINY))
                    u = jnp.maximum(1.0 - q, 0.0)
                    slope = near_s[f, 4 * slots + b, t + e][None] * (u * u * u)
                    slopes_ref[t * 5 + e, f, b] = slope
                    dens = dens + slope * (u * (1.25 - u))
                    slope_sum = slope_sum + slope
                    dvx = near_s[f, 2 * slots + b, t + e][None] - own_vx
                    dvy = near_s[f, 3 * slots + b, t + e][None] - own_vy
                    inflow = inflow + slope * (dvx * dx + dvy * dy)
            return dens, inflow, slope_sum

        if len(shifts) == 1:
            for e in range(5):
                sums = along(e, sums)
            return sums
        return lax.fori_loop(0, 5, along, sums)

    def finish(t, sums):
        dens, inflow, slope_sum = sums
        density = BACKGROUND + dens * (4.0 * KERNEL_NORM / SLOPE_NORM)
        inverse = 1.0 / density
        source = inflow * inverse * (-2.0 / TIME_STEP)
        first = source * over_middle[None]
        own_ref[0, t] = inverse
        own_ref[1, t] = DIAGONAL_SHIFT + 2.0 * inverse * slope_sum
        own_ref[2, t] = source
        own_ref[3, t] = first
        put_field(0, t, first)

    def flow_start(t):
        for n, value in enumerate(flow(t, (2,), (zero, zero, zero))):
            sums_ref[n, t] = value

    def flow_beside(t):
        sums = tuple(sums_ref[n, t] for n in range(3))
        finish(t, flow(t, (0, 1, 3, 4), sums))

    def flow_whole(t):
        finish(t, flow(t, (0, 1, 2, 3, 4), (zero, zero, zero)))

    inner_lines(flow_start)
    receive(0, (2, 3))
    spread_lines(0, near_s, inside, beside)
    inner_lines(flow_beside)
    receive(0, (0, 1, 4, 5, 6, 7))
    spread_lines(0, near_s, outside, everywhere)
    outer_lines(flow_whole)

    def gather(t, low_e, high_e, sums):
        def along(e, totals):
            totals = list(totals)
            for f in range(5):
                for b in range(slots):
                    near = near_p[f, b, t + e][None]
                    totals[b % 2] = totals[b % 2] + slopes_ref[t * 5 + e, f, b] * near
            return tuple(totals)

        return lax.fori_loop(low_e, high_e, along, sums)

    def push_part(t, low_e, high_e, sums):
        solved = own_ref[3, t]

        def along(e, sums):
            push_x, push_y, push = sums
            shift = 0.5 * jnp.asarray(e - 2, jnp.float32)
            for f in range(5):
                for b in range(slots):
                    part = slopes_ref[t * 5 + e, f, b] * (near_p[f, b, t + e][None] - solved)
                    push = push + part
                    push_x = push_x + part * (near_s[f, b, t + e] + shift)[None]
                    push_y = push_y + part * near_s[f, slots + b, t + e][None]
            return push_x, push_y, push

        return lax.fori_loop(low_e, high_e, along, sums)

    def sweep(number, count, part, finish):
        start = (zero,) * count
        outer = (0, 1, steps - 2, steps - 1)
        pack(field_e.at[number], field_cs.at[number])
        send(number + 1)
        spread_lines(number + 1, near_p, inside, (0,))
        receive(number + 1, (2, 3))
        spread_lines(number + 1, near_p, inside, beside)
        inner_lines(lambda t: finish(t, part(t, 0, 5, start)))
        for t in outer:
            sums = part(t, max(0, 2 - t), min(5, steps + 2 - t), start)
            for n, value in enumerate(sums):
                sums_ref[n, t] = value
        receive(number + 1, (0, 1, 4, 5, 6, 7))
        spread_lines(number + 1, near_p, outside, everywhere)
        for t in outer:
            sums = tuple(sums_ref[n, t] for n in range(count))
            if t < 2:
                sums = part(t, 0, 2 - t, sums)
            else:
                sums = part(t, steps + 2 - t, 5, sums)
            finish(t, sums)

    def second_step(t, sums):
        field = own_ref[3, t]
        residual = own_ref[2, t] - (own_ref[1, t] * field - 2.0 * own_ref[0, t] * (sums[0] + sums[1]))
        second = keep_one[None] * field + gain_one[None] * residual
        own_ref[2, t] = residual
        own_ref[4, t] = second
        put_field(1, t, second)

    def third_step(t, sums):
        field = own_ref[4, t]
        residual = own_ref[2, t] - (own_ref[1, t] * field - 2.0 * own_ref[0, t] * (sums[0] + sums[1]))
        third = keep_two[None] * field + gain_two[None] * residual
        solved = own_ref[3, t] + field + third
        own_ref[3, t] = solved
        put_field(2, t, solved)

    def kick(t, sums):
        own_x = own_state(0, t)
        own_y = own_state(1, t)
        solved = own_ref[3, t]
        push_x, push_y, push = sums
        scale = own_ref[0, t] * (2.0 * TIME_STEP)
        new_x = own_state(2, t) - scale * (push_x - own_x * push)
        new_y = own_state(3, t) - scale * (push_y - own_y * push)
        live = counts_ref[pl.ds(t, 8, stride=8), :]
        for slot in range(slots):
            occupied = jnp.where(live > slot, 1.0, 0.0).astype(jnp.float32)
            nv_ref[0, slot, pl.ds(t, 8, stride=8), :] = occupied * new_x[slot]
            nv_ref[1, slot, pl.ds(t, 8, stride=8), :] = occupied * new_y[slot]
            press_ref[slot, pl.ds(t, 8, stride=8), :] = occupied * solved[slot]

    sweep(0, 2, gather, second_step)
    sweep(1, 2, gather, third_step)
    sweep(2, 3, push_part, kick)
    for number in range(4):
        drain(number)


def on_device(rows, cols, offsets, velocity, mass, counts, spectrum_low, spectrum_high):
    slots, height, width = mass.shape
    assert height % 16 == 0 and height >= 48 and width % 128 == 0
    steps = height // 8
    planes = 5 * slots
    vmem = pl.BlockSpec(memory_space=pltpu.VMEM)
    hbm = pl.BlockSpec(memory_space=pltpu.HBM)

    def room(*shape):
        return pltpu.VMEM(shape, jnp.float32)

    return pl.pallas_call(
        functools.partial(kernel, rows, cols),
        out_shape=(
            jax.ShapeDtypeStruct(velocity.shape, jnp.float32),
            jax.ShapeDtypeStruct(mass.shape, jnp.float32),
        ),
        in_specs=[hbm] * 6,
        out_specs=(vmem, vmem),
        scratch_shapes=[
            room(*offsets.shape),
            room(*velocity.shape),
            room(*mass.shape),
            pltpu.VMEM(counts.shape, jnp.int32),
            pltpu.SMEM(spectrum_low.shape, jnp.float32),
            pltpu.SMEM(spectrum_high.shape, jnp.float32),
            room(3, steps, slots, 8, width),
            pltpu.SemaphoreType.DMA((6,)),
            room(planes, height + 16, width),
            room(2, height, width),
            room(2, height + 16, width),
            room(3, slots, height + 16, width),
            room(3, 2, height, width),
            room(3, 2, height + 16, width),
            room(5, planes, steps + 4, 8, width),
            room(5, slots, steps + 4, 8, width),
            room(steps * 5, 5, slots, slots, 8, width),
            room(5, steps, slots, 8, width),
            pltpu.SemaphoreType.DMA((4, 8)),
            pltpu.SemaphoreType.DMA((4, 8)),
        ],
        compiler_params=pltpu.CompilerParams(
            collective_id=0, has_side_effects=True, vmem_limit_bytes=66_500_000
        ),
        name="sph_step",
    )(offsets, velocity, mass, counts, spectrum_low, spectrum_high)


def solution(mesh):
    placed = (
        P(None, None, "row", "col"),
        P(None, None, "row", "col"),
        P(None, "row", "col"),
        P("row", "col"),
        P(),
        P(),
    )
    return jax.shard_map(
        functools.partial(on_device, mesh.shape["row"], mesh.shape["col"]),
        mesh=mesh,
        in_specs=placed,
        out_specs=(P(None, None, "row", "col"), P(None, "row", "col")),
        check_vma=False,
    )
```

profile of v0, /device:TPU:0, one launch (start us, length us, event | category | flops | bytes accessed | tf_op | source)
XLA Modules:
  0.0 42.4 jit_solution(16355366329206572574)
XLA Ops:
  1.9 38.1 %sph_step.1 = (f32[2,4,64,128]{3,2,1,0:T(8,128)}, f32[4,64,128]{2,1,0:T(8,128)}) custom-call(f32[2,4,64,128]{3,2,1,0:T(8,128)} %off_hbm.1, f32[2,4,64,128]{3,2,1,0:T(8,128)} %vel_hbm.1, f32[4,64,128]{2,1,0:T(8,128)} %mass_hbm.1, s32[64,128]{1,0:T(8,128)} %counts_hbm.1, f32[1]{0:T(128)S(6)} %copy.10.low_hbm, f32[1]{0:T(128)S(6)} %copy.11.high_hbm), custom_call_target="tpu_custom_call" | custom-call | tf_op jit(solution)/shard_map/sph_step/pallas_call | solution.py:445
  40.1 0.0 copy-start
  40.1 1.7 %copy.12 = f32[2,4,64,128]{3,2,1,0:T(8,128)} copy(f32[2,4,64,128]{3,2,1,0:T(8,128)} %get-tuple-element.4) | data formatting | bytes 524288
  41.8 0.0 copy-done
  41.8 0.7 %copy.13 = f32[4,64,128]{2,1,0:T(8,128)} copy(f32[4,64,128]{2,1,0:T(8,128)S(1)} %copy-done) | data formatting | bytes 262144
Async XLA Ops:
  40.1 1.7 %copy-start = (f32[4,64,128]{2,1,0:T(8,128)S(1)}, f32[4,64,128]{2,1,0:T(8,128)}, u32[]{:S(2)}) copy-start(f32[4,64,128]{2,1,0:T(8,128)} %get-tuple-element.5) | copy-start | bytes 393220
where the time goes:
time: 42.6 us; the launch traced here: 42.4 us
  Pallas kernels  38.1 us (89%)
  local copies, waits for them, and re-layouts  2.37 us (6%)
  between operations  1.94 us (5%)
    pallas_call x1, Pallas kernels, on_device(): pl.pallas_call(functools.partial(kernel, rows, cols), out_shape=(jax.Shap...  38.1 us
    unnamed x4, local copies, waits for them, and re-layouts  2.37 us

commit v1 on v0

--- a/solution.py
+++ b/solution.py
@@ -14,6 +14,8 @@
 BACKGROUND = 0.5 * KERNEL_NORM
 DIAGONAL_SHIFT = 1.0
 TINY = 1e-30
+VMEM_BYTES = 67_043_328
+SPARE = 8192
 MESH = pl.DeviceIdType.MESH
 DIRECTIONS = ((1, 0), (-1, 0), (0, 1), (0, -1), (1, 1), (-1, 1), (1, -1), (-1, -1))
 
@@ -436,6 +438,7 @@
     assert height % 16 == 0 and height >= 48 and width % 128 == 0
     steps = height // 8
     planes = 5 * slots
+    results = 4 * (velocity.size + mass.size)
     vmem = pl.BlockSpec(memory_space=pltpu.VMEM)
     hbm = pl.BlockSpec(memory_space=pltpu.HBM)
 
@@ -445,8 +448,8 @@
     return pl.pallas_call(
         functools.partial(kernel, rows, cols),
         out_shape=(
-            jax.ShapeDtypeStruct(velocity.shape, jnp.float32),
-            jax.ShapeDtypeStruct(mass.shape, jnp.float32),
+            pltpu.VMEM(velocity.shape, jnp.float32),
+            pltpu.VMEM(mass.shape, jnp.float32),
         ),
         in_specs=[hbm] * 6,
         out_specs=(vmem, vmem),
@@ -473,7 +476,7 @@
             pltpu.SemaphoreType.DMA((4, 8)),
         ],
         compiler_params=pltpu.CompilerParams(
-            collective_id=0, has_side_effects=True, vmem_limit_bytes=66_500_000
+            collective_id=0, has_side_effects=True, vmem_limit_bytes=VMEM_BYTES - results - SPARE
         ),
         name="sph_step",
     )(offsets, velocity, mass, counts, spectrum_low, spectrum_high)

time: 42.6 us -> 40.8 us (0.958)
  local copies, waits for them, and re-layouts: 2.37 us -> 1.36 us
  Pallas kernels: 38.1 us -> 37.4 us
    unnamed x4 -> x2, local copies, waits for them, and re-layouts: 2.37 us -> 1.36 us
    pallas_call x1, Pallas kernels: 38.1 us -> 37.4 us  [on_device(): pl.pallas_call(functools.partial(kernel, rows, cols), out_shape=(pltpu.VM...]
where the time goes in v1:
time: 40.8 us; the launch traced here: 40.6 us
  Pallas kernels  37.4 us (92%)
  between operations  1.93 us (5%)
  local copies, waits for them, and re-layouts  1.36 us (3%)
    pallas_call x1, Pallas kernels, on_device(): pl.pallas_call(functools.partial(kernel, rows, cols), out_shape=(pltpu.VM...  37.4 us
    unnamed x2, local copies, waits for them, and re-layouts  1.36 us

profile of v1, /device:TPU:0, one launch (start us, length us, event | category | flops | bytes accessed | tf_op | source)
XLA Modules:
  0.0 40.6 jit_solution(7908859849192703724)
XLA Ops:
  1.9 37.4 %sph_step.1 = (f32[2,4,64,128]{3,2,1,0:T(8,128)S(1)}, f32[4,64,128]{2,1,0:T(8,128)S(1)}) custom-call(f32[2,4,64,128]{3,2,1,0:T(8,128)} %off_hbm.1, f32[2,4,64,128]{3,2,1,0:T(8,128)} %vel_hbm.1, f32[4,64,128]{2,1,0:T(8,128)} %mass_hbm.1, s32[64,128]{1,0:T(8,128)} %counts_hbm.1, f32[1]{0:T(128)S(6)} %copy.12.low_hbm, f32[1]{0:T(128)S(6)} %copy.13.high_hbm), custom_call_target="tpu_custom_call" | custom-call | tf_op jit(solution)/shard_map/sph_step/pallas_call | solution.py:448
  39.3 0.7 %copy.10 = f32[2,4,64,128]{3,2,1,0:T(8,128)} copy(f32[2,4,64,128]{3,2,1,0:T(8,128)S(1)} %get-tuple-element.2) | data formatting | bytes 524288
  40.0 0.7 %copy.11 = f32[4,64,128]{2,1,0:T(8,128)} copy(f32[4,64,128]{2,1,0:T(8,128)S(1)} %get-tuple-element.3) | data formatting | bytes 262144

commit v2 on v1

v2 whole, which is shorter than its diff:
```python
import functools
import math

import jax
import jax.numpy as jnp
from jax import lax
from jax.experimental import pallas as pl
from jax.experimental.pallas import tpu as pltpu
from jax.sharding import PartitionSpec as P

TIME_STEP = 0.1
KERNEL_NORM = 7.0 / (4.0 * math.pi)
SLOPE_NORM = 20.0 * KERNEL_NORM / 4.0
BACKGROUND = 0.5 * KERNEL_NORM
DIAGONAL_SHIFT = 1.0
REACH = 4.0 / 3.0
CELL = REACH / 2.0
VMEM_BYTES = 67_043_328
SPARE = 8192
MESH = pl.DeviceIdType.MESH
DIRECTIONS = ((1, 0), (-1, 0), (0, 1), (0, -1), (1, 1), (-1, 1), (1, -1), (-1, -1))


def kernel(
    rows,
    cols,
    off_hbm,
    vel_hbm,
    mass_hbm,
    counts_hbm,
    low_hbm,
    high_hbm,
    nv_ref,
    press_ref,
    off_ref,
    vel_ref,
    mass_ref,
    counts_ref,
    low_ref,
    high_ref,
    input_sem,
    tile_ref,
    above_ref,
    edge_ref,
    beside_ref,
    bend_ref,
    corner_ref,
    near_ref,
    around_ref,
    slopes_ref,
    moment_ref,
    own_ref,
    send_sem,
    recv_sem,
):
    slots, height, width = mass_hbm.shape
    steps = height // 8
    span = width // steps
    strip, corners, tops = steps, steps + 1, steps + 2
    planes = 5 * slots
    batch = width // span
    my_row = lax.axis_index("row")
    my_col = lax.axis_index("col")

    def exists(dr, dc):
        answer = None
        for shift, place, length in ((dr, my_row, rows), (dc, my_col, cols)):
            if shift == 0:
                continue
            test = place + shift < length if shift > 0 else place + shift >= 0
            answer = test if answer is None else jnp.logical_and(answer, test)
        return answer

    lane = lax.broadcasted_iota(jnp.int32, (8, width), 1)
    line = lax.broadcasted_iota(jnp.int32, (8, width), 0)
    place = lane % span
    block = ((lane + span // 2) % width) // span
    left_half = place < span // 2
    inverse_at, diagonal_at, residual_at, moment_at, sum_at, step_at = 0, 1, 2, 3, 5, 6

    loads = [
        pltpu.make_async_copy(source, target, input_sem.at[n])
        for n, (source, target) in enumerate(
            (
                (counts_hbm, counts_ref),
                (vel_hbm, vel_ref),
                (off_hbm, off_ref),
                (mass_hbm, mass_ref),
                (low_hbm, low_ref),
                (high_hbm, high_ref),
            )
        )
    ]
    for load in loads:
        load.start()

    barrier = pltpu.get_barrier_semaphore()
    for dr, dc in DIRECTIONS:

        @pl.when(exists(dr, dc))
        def _(dr=dr, dc=dc):
            pl.semaphore_signal(
                barrier, inc=1, device_id=(my_row + dr, my_col + dc), device_id_type=MESH
            )

    for side, dr in ((0, -1), (1, 1)):

        @pl.when(jnp.logical_not(exists(dr, 0)))
        def _(side=side):
            above_ref[side] = jnp.zeros(above_ref.shape[1:], jnp.float32)

    for side, dc in ((0, -1), (1, 1)):

        @pl.when(jnp.logical_not(exists(0, dc)))
        def _(side=side):
            beside_ref[side] = jnp.zeros(beside_ref.shape[1:], jnp.float32)

        for level, dr in ((0, -1), (1, 1)):

            @pl.when(jnp.logical_not(exists(dr, dc)))
            def _(side=side, level=level):
                corner_ref[side, level] = jnp.zeros(corner_ref.shape[2:], jnp.float32)

    for load in loads:
        load.wait()

    def particles(window, put):
        live = counts_ref[window, :]
        for slot in range(slots):
            occupied = jnp.where(live > slot, 1.0, 0.0).astype(jnp.float32)
            for axis in range(2):
                speed = vel_ref[axis, slot, window, :]
                place = off_ref[axis, slot, window, :] + TIME_STEP * speed
                put(axis * slots + slot, CELL * place)
                put((2 + axis) * slots + slot, speed)
            weight = mass_ref[slot, window, :] * occupied
            put(4 * slots + slot, (SLOPE_NORM / REACH**3) * weight)

    def own_tile(s, carry):
        window = pl.ds(pl.multiple_of(8 * s, 8), 8)

        def put_tile(plane, value):
            tile_ref[plane, window, :] = value

        particles(window, put_tile)
        return carry

    lax.fori_loop(0, steps, own_tile, 0)

    def lane_roll(value, shift):
        shift = shift % width
        return pltpu.roll(value, shift, 1) if shift else value

    def under(value, shift):
        return pltpu.roll(value, shift % 8, 0)

    def edges(plane):
        packed = tile_ref[plane, 0:8, :]
        for s in range(1, steps):
            moved = lane_roll(tile_ref[plane, 8 * s : 8 * s + 8, :], span * s)
            packed = jnp.where(block == s, moved, packed)
        return packed

    def each_plane(work):
        def body(index, carry):
            for n in range(slots):
                work(index * slots + n)
            return carry

        lax.fori_loop(0, planes // slots, body, 0)

    def pack(plane):
        edge_ref[plane] = edges(plane)

    each_plane(pack)

    for level, home in ((0, steps - 1), (1, 0)):
        for g in range(bend_ref.shape[1]):
            packed = None
            for n in range(min(batch, planes - g * batch)):
                moved = lane_roll(edge_ref[g * batch + n], span * (n - home))
                packed = moved if packed is None else jnp.where(block == n, moved, packed)
            bend_ref[level, g] = packed

    def copy(way):
        dr, dc = DIRECTIONS[way]
        theirs = 0 if dc > 0 else 1
        if dc == 0 and dr > 0:
            source, target = tile_ref.at[:, height - 8 : height, :], above_ref.at[0]
        elif dc == 0:
            source, target = tile_ref.at[:, 0:8, :], above_ref.at[1]
        elif dr == 0:
            source, target = edge_ref, beside_ref.at[theirs]
        else:
            level = 0 if dr > 0 else 1
            source, target = bend_ref.at[level], corner_ref.at[theirs, level]
        return pltpu.make_async_remote_copy(
            src_ref=source,
            dst_ref=target,
            send_sem=send_sem.at[way],
            recv_sem=recv_sem.at[way],
            device_id=(my_row + dr, my_col + dc),
            device_id_type=MESH,
        )

    tall = 1 + jnp.where(my_row > 0, 1, 0) + jnp.where(my_row + 1 < rows, 1, 0)
    wide = 1 + jnp.where(my_col > 0, 1, 0) + jnp.where(my_col + 1 < cols, 1, 0)
    pl.semaphore_wait(barrier, tall * wide - 1)
    for way in (4, 5, 6, 7, 2, 3, 0, 1):

        @pl.when(exists(*DIRECTIONS[way]))
        def _(way=way):
            copy(way).start()

    def own_line(plane):
        for t in range(steps):
            value = tile_ref[plane, pl.ds(t, 8, stride=8), :]
            for f in range(5):
                near_ref[f, plane, t + 2] = lane_roll(value, 2 - f)

    each_plane(own_line)

    def near_line(t):
        return lambda e, f, plane: near_ref[f, plane, t + e]

    def near_around(n):
        return lambda e, f, plane: around_ref[n, e, f, plane]

    def own(near, first):
        return jnp.stack([near(2, 2, first * slots + slot) for slot in range(slots)])

    zero = jnp.zeros((slots, 8, width), jnp.float32)
    start = (zero,) * 5

    def flow(x, near, low_e, high_e, sums, moments):
        own_x = own(near, 0)
        own_y = own(near, 1)

        def along(e, sums):
            slope_sum, dens, flux, sum_x, sum_y = sums
            base_x = own_x - CELL * jnp.asarray(e - 2, jnp.float32)
            for f in range(5):
                base_y = own_y - CELL * (f - 2) if f != 2 else own_y
                for b in range(slots):
                    dx = near(e, f, b)[None] - base_x
                    dy = near(e, f, slots + b)[None] - base_y
                    square = dx * dx + dy * dy
                    inverse = lax.rsqrt(square)
                    dist = lax.rsqrt(inverse * inverse)
                    u = jnp.maximum(REACH - dist, 0.0)
                    slope = (u * u) * (near(e, f, 4 * slots + b)[None] * u)
                    slopes_ref[x * 5 + e, f, b] = slope
                    slope_sum = slope_sum + slope
                    dens = dens + slope * (dist - square)
                    moment_x = slope * dx
                    moment_y = slope * dy
                    if moments:
                        moment_ref[0, x * 5 + e, f, b] = moment_x
                        moment_ref[1, x * 5 + e, f, b] = moment_y
                    flux = flux + moment_x * near(e, f, 2 * slots + b)[None]
                    flux = flux + moment_y * near(e, f, 3 * slots + b)[None]
                    sum_x = sum_x + moment_x
                    sum_y = sum_y + moment_y
            return slope_sum, dens, flux, sum_x, sum_y

        return lax.fori_loop(low_e, high_e, along, sums)

    def save(x, sums):
        for n, value in enumerate(sums):
            own_ref[n, x] = value

    def saved(x):
        return tuple(own_ref[n, x] for n in range(5))

    def each(first, last, work):
        def body(x, carry):
            work(x)
            return carry

        lax.fori_loop(first, last, body, 0)

    def flow_inner(t):
        low_e = jnp.maximum(0, 2 - t)
        high_e = jnp.minimum(5, steps + 2 - t)
        save(t, flow(t, near_line(t), low_e, high_e, start, True))

    def flow_outer(index):
        t = index + (index // 2) * (steps - 4)
        low_e = jnp.where(t < 2, 0, steps + 2 - t)
        high_e = jnp.where(t < 2, 2 - t, 5)
        save(t, flow(t, near_line(t), low_e, high_e, saved(t), True))

    each(0, steps, flow_inner)

    for way in range(8):
        dr, dc = DIRECTIONS[way]

        @pl.when(exists(-dr, -dc))
        def _(way=way):
            copy(way).wait_recv()

    def ring(plane, top, bottom):
        for f in range(5):
            above, below = lane_roll(top, 2 - f), lane_roll(bottom, 2 - f)
            first, second = near_ref[f, plane, 2], near_ref[f, plane, 3]
            before, last = near_ref[f, plane, steps], near_ref[f, plane, steps + 1]
            near_ref[f, plane, 0] = jnp.where(line == 0, under(above, 2), under(before, 1))
            near_ref[f, plane, 1] = jnp.where(line == 0, under(above, 1), under(last, 1))
            near_ref[f, plane, steps + 2] = jnp.where(line == 7, under(below, 7), under(first, 7))
            near_ref[f, plane, steps + 3] = jnp.where(line == 7, under(below, 6), under(second, 7))
            around_ref[2, 0, f, plane] = under(above, 2)
            around_ref[2, 1, f, plane] = under(above, 1)
            around_ref[2, 2, f, plane] = above
            around_ref[2, 3, f, plane] = jnp.where(line == 7, under(first, 7), under(above, 7))
            beyond = jnp.where(line == 7, under(second, 7), under(above, 6))
            around_ref[2, 4, f, plane] = jnp.where(line == 6, under(first, 6), beyond)
            beyond = jnp.where(line == 1, under(last, 2), under(below, 2))
            around_ref[3, 0, f, plane] = jnp.where(line == 0, under(before, 1), beyond)
            around_ref[3, 1, f, plane] = jnp.where(line == 0, under(last, 1), under(below, 1))
            around_ref[3, 2, f, plane] = below
            around_ref[3, 3, f, plane] = under(below, 7)
            around_ref[3, 4, f, plane] = under(below, 6)

    def widen(plane, inner, outer):
        for f in range(5):
            mine = (lane + (span + 2 - f)) % span < span // 2
            here = lane_roll(jnp.where(mine, *inner), 2 - f)
            bend = lane_roll(jnp.where(mine, *outer), 2 - f)
            after = jnp.where(lane >= width - span, bend, lane_roll(here, -span))
            ahead = jnp.where(lane < span, bend, lane_roll(here, span))
            for n, value, up, down in ((0, here, after, ahead), (1, bend, here, here)):
                around_ref[n, 0, f, plane] = under(jnp.where(line >= 6, down, value), 2)
                around_ref[n, 1, f, plane] = under(jnp.where(line >= 7, down, value), 1)
                around_ref[n, 2, f, plane] = value
                around_ref[n, 3, f, plane] = under(jnp.where(line < 1, up, value), 7)
                around_ref[n, 4, f, plane] = under(jnp.where(line < 2, up, value), 6)

    def fold(top, bottom):
        return jnp.where(block == 0, top, lane_roll(bottom, span * (steps - 1)))

    def arrive(plane, g, n):
        top, bottom = above_ref[0, plane], above_ref[1, plane]
        ring(plane, top, bottom)

        def strips(mine, theirs):
            left = lane_roll(jnp.where(left_half, mine, theirs), 6)
            right = lane_roll(jnp.where(left_half, theirs, mine), 10)
            return left, right

        inner = jnp.where(left_half, beside_ref[1, plane], beside_ref[0, plane])
        ends = [jnp.where(left_half, corner_ref[1, level, g], corner_ref[0, level, g]) for level in (0, 1)]
        outer = fold(lane_roll(ends[0], -span * n), lane_roll(ends[1], -span * n))
        widen(plane, strips(edge_ref[plane], inner), strips(fold(top, bottom), outer))

    def arrive_some(index, carry):
        g = index // 2
        for half in range(2):

            @pl.when(index % 2 == half)
            def _(half=half):
                for n in range(slots):
                    arrive(index * slots + n, g, half * slots + n)

        return carry

    lax.fori_loop(0, planes // slots, arrive_some, 0)

    each(0, 4, flow_outer)
    save(strip, flow(strip, near_around(0), 0, 5, start, True))
    each(1, 4, lambda n: save(steps + n, flow(steps + n, near_around(n), 0, 5, start, False)))

    full = (8, width)
    low = jnp.broadcast_to(low_ref[0], full)
    high = jnp.broadcast_to(high_ref[0], full)
    middle = 0.5 * (high + low)
    radius = 0.5 * (high - low)
    quotient = middle / radius
    factor_zero = 1.0 / quotient
    factor_one = 1.0 / (2.0 * quotient - factor_zero)
    factor_two = 1.0 / (2.0 * quotient - factor_one)
    over_middle = 1.0 / middle
    keep_one = factor_one * factor_zero
    keep_two = factor_two * factor_one
    gain_one = 2.0 * factor_one / radius
    gain_two = 2.0 * factor_two / radius

    def everyone(work):
        each(0, steps, lambda t: work(t, near_line(t)))
        each(0, 4, lambda n: work(steps + n, near_around(n)))

    def first_step(x, near):
        slope_sum, dens, flux, sum_x, sum_y = saved(x)
        density = BACKGROUND + (KERNEL_NORM / SLOPE_NORM) * (slope_sum + (4.0 / REACH**2) * dens)
        inverse = 1.0 / density
        inflow = flux - own(near, 2) * sum_x - own(near, 3) * sum_y
        source = inflow * inverse * (-1.0 / (CELL * TIME_STEP))
        own_ref[inverse_at, x] = inverse
        own_ref[diagonal_at, x] = DIAGONAL_SHIFT + 2.0 * inverse * slope_sum
        own_ref[residual_at, x] = source
        own_ref[sum_at, x] = source * over_middle[None]

    def turn(value):
        return jnp.where(left_half, lane_roll(value, -2), lane_roll(value, 2))

    def mend(value, turned, s):
        outermost = (lane < 2) | (lane >= width - 2)
        return jnp.where(outermost, lane_roll(turned, -span * s - span // 2), value)

    def refresh(at):
        for slot in range(slots):
            for t in range(steps):
                tile_ref[slot, pl.ds(t, 8, stride=8), :] = own_ref[at, t, slot]
            inner, outer = own_ref[at, strip, slot], own_ref[at, corners, slot]
            turned = turn(inner)
            for s in range(steps):
                window = slice(8 * s, 8 * s + 8)
                tile_ref[slot, window, :] = mend(tile_ref[slot, window, :], turned, s)
            turned = turn(outer)
            top = mend(own_ref[at, tops, slot], turned, 0)
            bottom = mend(own_ref[at, tops + 1, slot], turned, steps - 1)
            own_line(slot)
            ring(slot, top, bottom)

            def strips(value, mine):
                left = jnp.where(left_half, value, lane_roll(mine, 6))
                right = jnp.where(left_half, lane_roll(mine, 10), value)
                return left, right

            widen(slot, strips(inner, edges(slot)), strips(outer, fold(top, bottom)))

    def gather(x, near):
        def along(e, totals):
            totals = list(totals)
            for f in range(5):
                for b in range(slots):
                    value = near(e, f, b)[None]
                    totals[b % 2] = totals[b % 2] + slopes_ref[x * 5 + e, f, b] * value
            return tuple(totals)

        even, odd = lax.fori_loop(0, 5, along, (zero, zero))
        return even + odd

    def improve(x, near, here):
        total = gather(x, near)
        change = own_ref[diagonal_at, x] * here - 2.0 * own_ref[inverse_at, x] * total
        residual = own_ref[residual_at, x] - change
        own_ref[residual_at, x] = residual
        return residual

    def second_step(x, near):
        here = own_ref[sum_at, x]
        own_ref[step_at, x] = keep_one[None] * here + gain_one[None] * improve(x, near, here)

    def third_step(x, near):
        here = own_ref[step_at, x]
        third = keep_two[None] * here + gain_two[None] * improve(x, near, here)
        own_ref[sum_at, x] = own_ref[sum_at, x] + here + third

    def push(x, near):
        def along(e, totals):
            push_x, push_y = totals
            for f in range(5):
                for b in range(slots):
                    value = near(e, f, b)[None]
                    push_x = push_x + moment_ref[0, x * 5 + e, f, b] * value
                    push_y = push_y + moment_ref[1, x * 5 + e, f, b] * value
            return push_x, push_y

        pushes = lax.fori_loop(0, 5, along, (zero, zero))
        solved = own_ref[sum_at, x]
        scale = own_ref[inverse_at, x] * (TIME_STEP / CELL)
        return [
            own(near, 2 + axis) - scale * (pushes[axis] - solved * own_ref[moment_at + axis, x])
            for axis in range(2)
        ]

    def kick_line(t):
        for axis, value in enumerate(push(t, near_line(t))):
            for slot in range(slots):
                nv_ref[axis, slot, pl.ds(t, 8, stride=8), :] = value[slot]

    def kick_ends():
        turned = [[turn(value[slot]) for slot in range(slots)] for value in push(strip, near_around(0))]
        for s in range(steps):
            window = slice(8 * s, 8 * s + 8)
            live = counts_ref[window, :]
            for slot in range(slots):
                occupied = jnp.where(live > slot, 1.0, 0.0).astype(jnp.float32)
                for axis in range(2):
                    value = mend(nv_ref[axis, slot, window, :], turned[axis][slot], s)
                    nv_ref[axis, slot, window, :] = occupied * value
                press_ref[slot, window, :] = occupied * tile_ref[slot, window, :]

    for way in range(8):

        @pl.when(exists(*DIRECTIONS[way]))
        def _(way=way):
            copy(way).wait_send()

    everyone(first_step)
    refresh(sum_at)
    everyone(second_step)
    refresh(step_at)
    everyone(third_step)
    refresh(sum_at)
    each(0, steps, kick_line)
    kick_ends()

def on_device(rows, cols, offsets, velocity, mass, counts, spectrum_low, spectrum_high):
    slots, height, width = mass.shape
    steps = height // 8
    span = width // steps
    assert height % 8 == 0 and steps == 8 and width % 128 == 0 and span == 16
    planes = 5 * slots
    bends = -(-planes * span // width)
    count = steps + 4
    results = 4 * (velocity.size + mass.size)
    vmem = pl.BlockSpec(memory_space=pltpu.VMEM)
    hbm = pl.BlockSpec(memory_space=pltpu.HBM)

    def room(*shape):
        return pltpu.VMEM(shape, jnp.float32)

    return pl.pallas_call(
        functools.partial(kernel, rows, cols),
        out_shape=(
            pltpu.VMEM(velocity.shape, jnp.float32),
            pltpu.VMEM(mass.shape, jnp.float32),
        ),
        in_specs=[hbm] * 6,
        out_specs=(vmem, vmem),
        scratch_shapes=[
            room(*offsets.shape),
            room(*velocity.shape),
            room(*mass.shape),
            pltpu.VMEM(counts.shape, jnp.int32),
            pltpu.SMEM(spectrum_low.shape, jnp.float32),
            pltpu.SMEM(spectrum_high.shape, jnp.float32),
            pltpu.SemaphoreType.DMA((6,)),
            room(planes, height, width),
            room(2, planes, 8, width),
            room(planes, 8, width),
            room(2, planes, 8, width),
            room(2, bends, 8, width),
            room(2, 2, bends, 8, width),
            room(5, planes, steps + 4, 8, width),
            room(4, 5, 5, planes, 8, width),
            room(count * 5, 5, slots, slots, 8, width),
            room(2, (steps + 1) * 5, 5, slots, slots, 8, width),
            room(7, count, slots, 8, width),
            pltpu.SemaphoreType.DMA((8,)),
            pltpu.SemaphoreType.DMA((8,)),
        ],
        compiler_params=pltpu.CompilerParams(
            collective_id=0,
            has_side_effects=True,
            vmem_limit_bytes=VMEM_BYTES - results - SPARE,
        ),
        name="sph_step",
    )(offsets, velocity, mass, counts, spectrum_low, spectrum_high)


def solution(mesh):
    placed = (
        P(None, None, "row", "col"),
        P(None, None, "row", "col"),
        P(None, "row", "col"),
        P("row", "col"),
        P(),
        P(),
    )
    return jax.shard_map(
        functools.partial(on_device, mesh.shape["row"], mesh.shape["col"]),
        mesh=mesh,
        in_specs=placed,
        out_specs=(P(None, None, "row", "col"), P(None, "row", "col")),
        check_vma=False,
    )
```

time: 40.8 us -> 36.6 us (0.90)
  the two profiles are of different devices: /device:TPU:0 before, /device:TPU:1 now
where the time goes in v2:
time: 36.6 us; the launch traced here: 36.4 us
  Pallas kernels  33.1 us (90%)
  between operations  1.93 us (5%)
  local copies, waits for them, and re-layouts  1.36 us (4%)
    pallas_call x1, Pallas kernels, on_device(): pl.pallas_call(functools.partial(kernel, rows, cols), out_shape=(pltpu.VM...  33.1 us
    unnamed x2, local copies, waits for them, and re-layouts  1.36 us

profile of v2, /device:TPU:1, one launch (start us, length us, event | category | flops | bytes accessed | tf_op | source)
XLA Modules:
  0.0 36.4 jit_solution(1520083566425817638)
XLA Ops:
  1.9 33.1 %sph_step.1 = (f32[2,4,64,128]{3,2,1,0:T(8,128)S(1)}, f32[4,64,128]{2,1,0:T(8,128)S(1)}) custom-call(f32[2,4,64,128]{3,2,1,0:T(8,128)} %off_hbm.1, f32[2,4,64,128]{3,2,1,0:T(8,128)} %vel_hbm.1, f32[4,64,128]{2,1,0:T(8,128)} %mass_hbm.1, s32[64,128]{1,0:T(8,128)} %counts_hbm.1, f32[1]{0:T(128)S(6)} %copy.12.low_hbm, f32[1]{0:T(128)S(6)} %copy.13.high_hbm), custom_call_target="tpu_custom_call" | custom-call | tf_op jit(solution)/shard_map/sph_step/pallas_call | solution.py:524
  35.1 0.7 %copy.10 = f32[2,4,64,128]{3,2,1,0:T(8,128)} copy(f32[2,4,64,128]{3,2,1,0:T(8,128)S(1)} %get-tuple-element.2) | data formatting | bytes 524288
  35.8 0.7 %copy.11 = f32[4,64,128]{2,1,0:T(8,128)} copy(f32[4,64,128]{2,1,0:T(8,128)S(1)} %get-tuple-element.3) | data formatting | bytes 262144

commit v3 on v2

--- a/solution.py
+++ b/solution.py
@@ -17,6 +17,7 @@
 CELL = REACH / 2.0
 VMEM_BYTES = 67_043_328
 SPARE = 8192
+EARLY = 2
 MESH = pl.DeviceIdType.MESH
 DIRECTIONS = ((1, 0), (-1, 0), (0, 1), (0, -1), (1, 1), (-1, 1), (1, -1), (-1, -1))
 
@@ -203,15 +204,6 @@
             device_id_type=MESH,
         )
 
-    tall = 1 + jnp.where(my_row > 0, 1, 0) + jnp.where(my_row + 1 < rows, 1, 0)
-    wide = 1 + jnp.where(my_col > 0, 1, 0) + jnp.where(my_col + 1 < cols, 1, 0)
-    pl.semaphore_wait(barrier, tall * wide - 1)
-    for way in (4, 5, 6, 7, 2, 3, 0, 1):
-
-        @pl.when(exists(*DIRECTIONS[way]))
-        def _(way=way):
-            copy(way).start()
-
     def own_line(plane):
         for t in range(steps):
             value = tile_ref[plane, pl.ds(t, 8, stride=8), :]
@@ -230,14 +222,15 @@
         return jnp.stack([near(2, 2, first * slots + slot) for slot in range(slots)])
 
     zero = jnp.zeros((slots, 8, width), jnp.float32)
-    start = (zero,) * 5
-
     def flow(x, near, low_e, high_e, sums, moments):
         own_x = own(near, 0)
         own_y = own(near, 1)
+        if not moments:
+            own_vx = own(near, 2)
+            own_vy = own(near, 3)
 
         def along(e, sums):
-            slope_sum, dens, flux, sum_x, sum_y = sums
+            sums = list(sums)
             base_x = own_x - CELL * jnp.asarray(e - 2, jnp.float32)
             for f in range(5):
                 base_y = own_y - CELL * (f - 2) if f != 2 else own_y
@@ -250,27 +243,43 @@
                     u = jnp.maximum(REACH - dist, 0.0)
                     slope = (u * u) * (near(e, f, 4 * slots + b)[None] * u)
                     slopes_ref[x * 5 + e, f, b] = slope
-                    slope_sum = slope_sum + slope
-                    dens = dens + slope * (dist - square)
-                    moment_x = slope * dx
-                    moment_y = slope * dy
+                    sums[0] = sums[0] + slope
+                    sums[1] = sums[1] + slope * (dist - square)
                     if moments:
-                        moment_ref[0, x * 5 + e, f, b] = moment_x
-                        moment_ref[1, x * 5 + e, f, b] = moment_y
+                        moment_ref[0, x * 5 + e, f, b] = slope * dx
+                        moment_ref[1, x * 5 + e, f, b] = slope * dy
+                    else:
+                        dvx = near(e, f, 2 * slots + b)[None] - own_vx
+                        dvy = near(e, f, 3 * slots + b)[None] - own_vy
+                        sums[2] = sums[2] + slope * (dvx * dx + dvy * dy)
+            return tuple(sums)
+
+        return lax.fori_loop(low_e, high_e, along, sums)
+
+    def stir(x, near):
+        def along(e, sums):
+            flux, sum_x, sum_y = sums
+            for f in range(5):
+                for b in range(slots):
+                    moment_x = moment_ref[0, x * 5 + e, f, b]
+                    moment_y = moment_ref[1, x * 5 + e, f, b]
                     flux = flux + moment_x * near(e, f, 2 * slots + b)[None]
                     flux = flux + moment_y * near(e, f, 3 * slots + b)[None]
                     sum_x = sum_x + moment_x
                     sum_y = sum_y + moment_y
-            return slope_sum, dens, flux, sum_x, sum_y
-
-        return lax.fori_loop(low_e, high_e, along, sums)
+            return flux, sum_x, sum_y
+
+        flux, sum_x, sum_y = lax.fori_loop(0, 5, along, (zero,) * 3)
+        own_ref[moment_at, x] = sum_x
+        own_ref[moment_at + 1, x] = sum_y
+        return flux - own(near, 2) * sum_x - own(near, 3) * sum_y
 
     def save(x, sums):
         for n, value in enumerate(sums):
             own_ref[n, x] = value
 
-    def saved(x):
-        return tuple(own_ref[n, x] for n in range(5))
+    def saved(x, count):
+        return tuple(own_ref[n, x] for n in range(count))
 
     def each(first, last, work):
         def body(x, carry):
@@ -282,15 +291,27 @@
     def flow_inner(t):
         low_e = jnp.maximum(0, 2 - t)
         high_e = jnp.minimum(5, steps + 2 - t)
-        save(t, flow(t, near_line(t), low_e, high_e, start, True))
+        save(t, flow(t, near_line(t), low_e, high_e, (zero,) * 2, True))
 
     def flow_outer(index):
         t = index + (index // 2) * (steps - 4)
         low_e = jnp.where(t < 2, 0, steps + 2 - t)
         high_e = jnp.where(t < 2, 2 - t, 5)
-        save(t, flow(t, near_line(t), low_e, high_e, saved(t), True))
-
-    each(0, steps, flow_inner)
+        save(t, flow(t, near_line(t), low_e, high_e, saved(t, 2), True))
+
+    each(0, EARLY, flow_inner)
+
+    tall = 1 + jnp.where(my_row > 0, 1, 0) + jnp.where(my_row + 1 < rows, 1, 0)
+    wide = 1 + jnp.where(my_col > 0, 1, 0) + jnp.where(my_col + 1 < cols, 1, 0)
+    pl.semaphore_wait(barrier, tall * wide - 1)
+    for way in (4, 5, 6, 7, 2, 3, 0, 1):
+
+        @pl.when(exists(*DIRECTIONS[way]))
+        def _(way=way):
+            copy(way).start()
+
+    each(EARLY, steps, flow_inner)
+
 
     for way in range(8):
         dr, dc = DIRECTIONS[way]
@@ -366,8 +387,8 @@
     lax.fori_loop(0, planes // slots, arrive_some, 0)
 
     each(0, 4, flow_outer)
-    save(strip, flow(strip, near_around(0), 0, 5, start, True))
-    each(1, 4, lambda n: save(steps + n, flow(steps + n, near_around(n), 0, 5, start, False)))
+    save(strip, flow(strip, near_around(0), 0, 5, (zero,) * 2, True))
+    each(1, 4, lambda n: save(steps + n, flow(steps + n, near_around(n), 0, 5, (zero,) * 3, False)))
 
     full = (8, width)
     low = jnp.broadcast_to(low_ref[0], full)
@@ -388,11 +409,9 @@
         each(0, steps, lambda t: work(t, near_line(t)))
         each(0, 4, lambda n: work(steps + n, near_around(n)))
 
-    def first_step(x, near):
-        slope_sum, dens, flux, sum_x, sum_y = saved(x)
+    def first_step(x, slope_sum, dens, inflow):
         density = BACKGROUND + (KERNEL_NORM / SLOPE_NORM) * (slope_sum + (4.0 / REACH**2) * dens)
         inverse = 1.0 / density
-        inflow = flux - own(near, 2) * sum_x - own(near, 3) * sum_y
         source = inflow * inverse * (-1.0 / (CELL * TIME_STEP))
         own_ref[inverse_at, x] = inverse
         own_ref[diagonal_at, x] = DIAGONAL_SHIFT + 2.0 * inverse * slope_sum
@@ -497,7 +516,9 @@
         def _(way=way):
             copy(way).wait_send()
 
-    everyone(first_step)
+    each(0, steps, lambda t: first_step(t, *saved(t, 2), stir(t, near_line(t))))
+    first_step(strip, *saved(strip, 2), stir(strip, near_around(0)))
+    each(1, 4, lambda n: first_step(steps + n, *saved(steps + n, 3)))
     refresh(sum_at)
     everyone(second_step)
     refresh(step_at)
@@ -514,14 +535,14 @@
     planes = 5 * slots
     bends = -(-planes * span // width)
     count = steps + 4
-    results = 4 * (velocity.size + mass.size)
+    room_out = 4 * (velocity.size + mass.size)
     vmem = pl.BlockSpec(memory_space=pltpu.VMEM)
     hbm = pl.BlockSpec(memory_space=pltpu.HBM)
 
     def room(*shape):
         return pltpu.VMEM(shape, jnp.float32)
 
-    return pl.pallas_call(
+    results = pl.pallas_call(
         functools.partial(kernel, rows, cols),
         out_shape=(
             pltpu.VMEM(velocity.shape, jnp.float32),
@@ -554,10 +575,33 @@
         compiler_params=pltpu.CompilerParams(
             collective_id=0,
             has_side_effects=True,
-            vmem_limit_bytes=VMEM_BYTES - results - SPARE,
+            vmem_limit_bytes=VMEM_BYTES - room_out - SPARE,
         ),
         name="sph_step",
     )(offsets, velocity, mass, counts, spectrum_low, spectrum_high)
+    return pl.pallas_call(
+        put_out,
+        out_shape=(
+            jax.ShapeDtypeStruct(velocity.shape, jnp.float32),
+            jax.ShapeDtypeStruct(mass.shape, jnp.float32),
+        ),
+        in_specs=[vmem] * 2,
+        out_specs=(hbm, hbm),
+        scratch_shapes=[pltpu.SemaphoreType.DMA((2,))],
+        compiler_params=pltpu.CompilerParams(vmem_limit_bytes=1 << 20),
+        name="put_out",
+    )(*results)
+
+
+def put_out(nv_ref, press_ref, nv_hbm, press_hbm, sem):
+    copies = [
+        pltpu.make_async_copy(nv_ref, nv_hbm, sem.at[0]),
+        pltpu.make_async_copy(press_ref, press_hbm, sem.at[1]),
+    ]
+    for copy in copies:
+        copy.start()
+    for copy in copies:
+        copy.wait()
 
 
 def solution(mesh):

time: 36.6 us -> 34.2 us (0.934)
  the two profiles are of different devices: /device:TPU:1 before, /device:TPU:0 now
where the time goes in v3:
time: 34.2 us; the launch traced here: 34 us
  Pallas kernels  32.1 us (94%)
  between operations  1.93 us (6%)
    pallas_call x1, Pallas kernels, on_device(): pl.pallas_call(functools.partial(kernel, rows, cols), out_shape=(pltpu.VM...  31.4 us
    pallas_call x1, Pallas kernels, on_device(): pl.pallas_call(put_out, out_shape=(jax.ShapeDtypeStruct(velocity.shape, j...  0.76 us

profile of v3, /device:TPU:0, one launch (start us, length us, event | category | flops | bytes accessed | tf_op | source)
XLA Modules:
  0.0 34.0 jit_solution(2878289209432853999)
XLA Ops:
  1.9 31.4 %sph_step.1 = (f32[2,4,64,128]{3,2,1,0:T(8,128)S(1)}, f32[4,64,128]{2,1,0:T(8,128)S(1)}) custom-call(f32[2,4,64,128]{3,2,1,0:T(8,128)} %off_hbm.1, f32[2,4,64,128]{3,2,1,0:T(8,128)} %vel_hbm.1, f32[4,64,128]{2,1,0:T(8,128)} %mass_hbm.1, s32[64,128]{1,0:T(8,128)} %counts_hbm.1, f32[1]{0:T(128)S(6)} %copy.8.low_hbm, f32[1]{0:T(128)S(6)} %copy.9.high_hbm), custom_call_target="tpu_custom_call" | custom-call | tf_op jit(solution)/shard_map/sph_step/pallas_call | solution.py:545
  33.3 0.8 %put_out.1 = (f32[2,4,64,128]{3,2,1,0:T(8,128)}, f32[4,64,128]{2,1,0:T(8,128)}) custom-call(f32[2,4,64,128]{3,2,1,0:T(8,128)S(1)} %get-tuple-element.4.nv_ref, f32[4,64,128]{2,1,0:T(8,128)S(1)} %get-tuple-element.5.press_ref), custom_call_target="tpu_custom_call" | custom-call | tf_op jit(solution)/shard_map/put_out/pallas_call | solution.py:582

commit v4 on v3

--- a/solution.py
+++ b/solution.py
@@ -162,6 +162,9 @@
             packed = jnp.where(block == s, moved, packed)
         return packed
 
+    def bias_of(index):
+        return jnp.where(index == 1, CELL, 0.0).astype(jnp.float32)
+
     def each_plane(work):
         def body(index, carry):
             for n in range(slots):
@@ -204,13 +207,22 @@
             device_id_type=MESH,
         )
 
-    def own_line(plane):
+    def shifted(value, f, bias):
+        moved = lane_roll(value, 2 - f)
+        return moved if bias is None or f == 2 else moved + bias * (f - 2.0)
+
+    def own_line(plane, bias):
         for t in range(steps):
             value = tile_ref[plane, pl.ds(t, 8, stride=8), :]
             for f in range(5):
-                near_ref[f, plane, t + 2] = lane_roll(value, 2 - f)
-
-    each_plane(own_line)
+                near_ref[f, plane, t + 2] = shifted(value, f, bias)
+
+    def own_lines(index, carry):
+        for n in range(slots):
+            own_line(index * slots + n, bias_of(index))
+        return carry
+
+    lax.fori_loop(0, planes // slots, own_lines, 0)
 
     def near_line(t):
         return lambda e, f, plane: near_ref[f, plane, t + e]
@@ -233,10 +245,9 @@
             sums = list(sums)
             base_x = own_x - CELL * jnp.asarray(e - 2, jnp.float32)
             for f in range(5):
-                base_y = own_y - CELL * (f - 2) if f != 2 else own_y
                 for b in range(slots):
                     dx = near(e, f, b)[None] - base_x
-                    dy = near(e, f, slots + b)[None] - base_y
+                    dy = near(e, f, slots + b)[None] - own_y
                     square = dx * dx + dy * dy
                     inverse = lax.rsqrt(square)
                     dist = lax.rsqrt(inverse * inverse)
@@ -320,9 +331,9 @@
         def _(way=way):
             copy(way).wait_recv()
 
-    def ring(plane, top, bottom):
+    def ring(plane, top, bottom, bias):
         for f in range(5):
-            above, below = lane_roll(top, 2 - f), lane_roll(bottom, 2 - f)
+            above, below = shifted(top, f, bias), shifted(bottom, f, bias)
             first, second = near_ref[f, plane, 2], near_ref[f, plane, 3]
             before, last = near_ref[f, plane, steps], near_ref[f, plane, steps + 1]
             near_ref[f, plane, 0] = jnp.where(line == 0, under(above, 2), under(before, 1))
@@ -342,11 +353,11 @@
             around_ref[3, 3, f, plane] = under(below, 7)
             around_ref[3, 4, f, plane] = under(below, 6)
 
-    def widen(plane, inner, outer):
+    def widen(plane, inner, outer, bias):
         for f in range(5):
             mine = (lane + (span + 2 - f)) % span < span // 2
-            here = lane_roll(jnp.where(mine, *inner), 2 - f)
-            bend = lane_roll(jnp.where(mine, *outer), 2 - f)
+            here = shifted(jnp.where(mine, *inner), f, bias)
+            bend = shifted(jnp.where(mine, *outer), f, bias)
             after = jnp.where(lane >= width - span, bend, lane_roll(here, -span))
             ahead = jnp.where(lane < span, bend, lane_roll(here, span))
             for n, value, up, down in ((0, here, after, ahead), (1, bend, here, here)):
@@ -359,9 +370,9 @@
     def fold(top, bottom):
         return jnp.where(block == 0, top, lane_roll(bottom, span * (steps - 1)))
 
-    def arrive(plane, g, n):
+    def arrive(plane, g, n, bias):
         top, bottom = above_ref[0, plane], above_ref[1, plane]
-        ring(plane, top, bottom)
+        ring(plane, top, bottom, bias)
 
         def strips(mine, theirs):
             left = lane_roll(jnp.where(left_half, mine, theirs), 6)
@@ -371,7 +382,7 @@
         inner = jnp.where(left_half, beside_ref[1, plane], beside_ref[0, plane])
         ends = [jnp.where(left_half, corner_ref[1, level, g], corner_ref[0, level, g]) for level in (0, 1)]
         outer = fold(lane_roll(ends[0], -span * n), lane_roll(ends[1], -span * n))
-        widen(plane, strips(edge_ref[plane], inner), strips(fold(top, bottom), outer))
+        widen(plane, strips(edge_ref[plane], inner), strips(fold(top, bottom), outer), bias)
 
     def arrive_some(index, carry):
         g = index // 2
@@ -380,7 +391,7 @@
             @pl.when(index % 2 == half)
             def _(half=half):
                 for n in range(slots):
-                    arrive(index * slots + n, g, half * slots + n)
+                    arrive(index * slots + n, g, half * slots + n, bias_of(index))
 
         return carry
 
@@ -437,15 +448,15 @@
             turned = turn(outer)
             top = mend(own_ref[at, tops, slot], turned, 0)
             bottom = mend(own_ref[at, tops + 1, slot], turned, steps - 1)
-            own_line(slot)
-            ring(slot, top, bottom)
+            own_line(slot, None)
+            ring(slot, top, bottom, None)
 
             def strips(value, mine):
                 left = jnp.where(left_half, value, lane_roll(mine, 6))
                 right = jnp.where(left_half, lane_roll(mine, 10), value)
                 return left, right
 
-            widen(slot, strips(inner, edges(slot)), strips(outer, fold(top, bottom)))
+            widen(slot, strips(inner, edges(slot)), strips(outer, fold(top, bottom)), None)
 
     def gather(x, near):
         def along(e, totals):

time: 34.2 us -> 33.7 us (0.985)
  Pallas kernels: 32.1 us -> 31.6 us
    pallas_call x1, Pallas kernels: 31.4 us -> 30.8 us  [on_device(): pl.pallas_call(functools.partial(kernel, rows, cols), out_shape=(pltpu.VM...]
where the time goes in v4:
time: 33.7 us; the launch traced here: 33.5 us
  Pallas kernels  31.6 us (94%)
  between operations  1.93 us (6%)
    pallas_call x1, Pallas kernels, on_device(): pl.pallas_call(functools.partial(kernel, rows, cols), out_shape=(pltpu.VM...  30.8 us
    pallas_call x1, Pallas kernels, on_device(): pl.pallas_call(put_out, out_shape=(jax.ShapeDtypeStruct(velocity.shape, j...  0.76 us

profile of v4, /device:TPU:0, one launch (start us, length us, event | category | flops | bytes accessed | tf_op | source)
XLA Modules:
  0.0 33.5 jit_solution(7924656270507903927)
XLA Ops:
  1.9 30.8 %sph_step.1 = (f32[2,4,64,128]{3,2,1,0:T(8,128)S(1)}, f32[4,64,128]{2,1,0:T(8,128)S(1)}) custom-call(f32[2,4,64,128]{3,2,1,0:T(8,128)} %off_hbm.1, f32[2,4,64,128]{3,2,1,0:T(8,128)} %vel_hbm.1, f32[4,64,128]{2,1,0:T(8,128)} %mass_hbm.1, s32[64,128]{1,0:T(8,128)} %counts_hbm.1, f32[1]{0:T(128)S(6)} %copy.8.low_hbm, f32[1]{0:T(128)S(6)} %copy.9.high_hbm), custom_call_target="tpu_custom_call" | custom-call | tf_op jit(solution)/shard_map/sph_step/pallas_call | solution.py:556
  32.8 0.8 %put_out.1 = (f32[2,4,64,128]{3,2,1,0:T(8,128)}, f32[4,64,128]{2,1,0:T(8,128)}) custom-call(f32[2,4,64,128]{3,2,1,0:T(8,128)S(1)} %get-tuple-element.4.nv_ref, f32[4,64,128]{2,1,0:T(8,128)S(1)} %get-tuple-element.5.press_ref), custom_call_target="tpu_custom_call" | custom-call | tf_op jit(solution)/shard_map/put_out/pallas_call | solution.py:593

commit v5 on v4

--- a/solution.py
+++ b/solution.py
@@ -310,18 +310,21 @@
         high_e = jnp.where(t < 2, 2 - t, 5)
         save(t, flow(t, near_line(t), low_e, high_e, saved(t, 2), True))
 
-    each(0, EARLY, flow_inner)
-
-    tall = 1 + jnp.where(my_row > 0, 1, 0) + jnp.where(my_row + 1 < rows, 1, 0)
-    wide = 1 + jnp.where(my_col > 0, 1, 0) + jnp.where(my_col + 1 < cols, 1, 0)
-    pl.semaphore_wait(barrier, tall * wide - 1)
-    for way in (4, 5, 6, 7, 2, 3, 0, 1):
-
-        @pl.when(exists(*DIRECTIONS[way]))
-        def _(way=way):
-            copy(way).start()
-
-    each(EARLY, steps, flow_inner)
+    def greet_and_flow(t):
+        @pl.when(t == EARLY)
+        def _():
+            tall = 1 + jnp.where(my_row > 0, 1, 0) + jnp.where(my_row + 1 < rows, 1, 0)
+            wide = 1 + jnp.where(my_col > 0, 1, 0) + jnp.where(my_col + 1 < cols, 1, 0)
+            pl.semaphore_wait(barrier, tall * wide - 1)
+            for way in (4, 5, 6, 7, 2, 3, 0, 1):
+
+                @pl.when(exists(*DIRECTIONS[way]))
+                def _(way=way):
+                    copy(way).start()
+
+        flow_inner(t)
+
+    each(0, steps, greet_and_flow)
 
 
     for way in range(8):

time: 33.7 us -> 33.9 us (level)
  no operation moved by 1% of the time
where the time goes in v5:
time: 33.9 us; the launch traced here: 33.7 us
  Pallas kernels  31.7 us (94%)
  between operations  1.93 us (6%)
    pallas_call x1, Pallas kernels, on_device(): pl.pallas_call(functools.partial(kernel, rows, cols), out_shape=(pltpu.VM...  31 us
    pallas_call x1, Pallas kernels, on_device(): pl.pallas_call(put_out, out_shape=(jax.ShapeDtypeStruct(velocity.shape, j...  0.76 us

profile of v5, /device:TPU:0, one launch (start us, length us, event | category | flops | bytes accessed | tf_op | source)
XLA Modules:
  0.0 33.7 jit_solution(4186622550253651914)
XLA Ops:
  1.9 31.0 %sph_step.1 = (f32[2,4,64,128]{3,2,1,0:T(8,128)S(1)}, f32[4,64,128]{2,1,0:T(8,128)S(1)}) custom-call(f32[2,4,64,128]{3,2,1,0:T(8,128)} %off_hbm.1, f32[2,4,64,128]{3,2,1,0:T(8,128)} %vel_hbm.1, f32[4,64,128]{2,1,0:T(8,128)} %mass_hbm.1, s32[64,128]{1,0:T(8,128)} %counts_hbm.1, f32[1]{0:T(128)S(6)} %copy.8.low_hbm, f32[1]{0:T(128)S(6)} %copy.9.high_hbm), custom_call_target="tpu_custom_call" | custom-call | tf_op jit(solution)/shard_map/sph_step/pallas_call | solution.py:559
  32.9 0.8 %put_out.1 = (f32[2,4,64,128]{3,2,1,0:T(8,128)}, f32[4,64,128]{2,1,0:T(8,128)}) custom-call(f32[2,4,64,128]{3,2,1,0:T(8,128)S(1)} %get-tuple-element.4.nv_ref, f32[4,64,128]{2,1,0:T(8,128)S(1)} %get-tuple-element.5.press_ref), custom_call_target="tpu_custom_call" | custom-call | tf_op jit(solution)/shard_map/put_out/pallas_call | solution.py:596
